TPU v7x, 32 devices: a whole 2x2x4 slice. The times are simulated.
32 devices in a mesh: outer: 4 (over y, core), row: 4 (over z), col: 2 (over x).
Axes of the slice: x: 2, y: 2, z: 4, core: 2. Of those that a mesh axis runs over, the one named last changes fastest.
Arguments:
- activations: bfloat16 [2048, 9216], P(('outer', 'col'), 'row'), may hold values from -13 to 13
- out_grads: bfloat16 [2048, 8192], P(('outer', 'row'), 'col'), may hold values from -13 to 13
- row_moment: float32 [9216], P(('row', 'outer')), may hold values from 0.3 to 3
- col_moment: float32 [8192], P('col'), may hold values from 0.3 to 3
Outputs:
- update: bfloat16 [9216, 8192], P(('row', 'outer'), 'col')
- new_row: float32 [9216], P(('row', 'outer'))
- new_col: float32 [8192], P('col')
All inputs are finite; a program needn't handle non-finite values.
Results may differ from a plain program's by a relative error of at most 0.001.
Values may be sent and summed in bfloat16 or wider, within the bound.
A program may use at most 128 MiB of HBM per device.

v0:
```python
import jax
import jax.numpy as jnp
from jax import lax
from jax.sharding import PartitionSpec as P

D = 9216
F = 8192
STEP = 2


def body(activations, out_grads, row_moment, col_moment):
    row_count = row_moment.shape[0]
    quarter = lax.axis_index("outer") * row_count
    token_count = activations.shape[0] * lax.axis_size("col") * lax.axis_size("outer")
    contract = (((0,), (0,)), ((), ()))
    grads_all = lax.all_gather(out_grads, ("outer", "row"), axis=0, tiled=True)
    columns = lax.dynamic_slice_in_dim(
        lax.all_gather(activations, ("outer", "col"), axis=0, tiled=True), quarter, row_count, 1
    )
    gradient = lax.dot_general(columns, grads_all, contract, preferred_element_type=jnp.float32)
    gradient = gradient * (1.0 / token_count**0.5)
    squares = gradient * gradient
    col_squares, old_total = lax.psum(
        (jnp.sum(squares, axis=0), jnp.sum(row_moment)), ("outer", "row")
    )
    row_squares, grad_total = lax.psum((jnp.sum(squares, axis=1), jnp.sum(col_squares)), "col")
    decay_rate = 1.0 - STEP ** (-0.8)
    new_row = decay_rate * row_moment + (1.0 - decay_rate) * row_squares / F
    new_col = decay_rate * col_moment + (1.0 - decay_rate) * col_squares / D
    moment_total = decay_rate * old_total + (1.0 - decay_rate) * grad_total / F
    factor = lax.rsqrt(new_row[:, None] * new_col[None, :] * (D / moment_total))
    update = (gradient * factor).astype(jnp.bfloat16)
    return (update, new_row, new_col)


def solution(mesh):
    return jax.shard_map(
        body,
        mesh=mesh,
        in_specs=(
            P(("outer", "col"), "row"),
            P(("outer", "row"), "col"),
            P(("row", "outer")),
            P("col"),
        ),
        out_specs=(P(("row", "outer"), "col"), P(("row", "outer")), P("col")),
        check_vma=False,
    )
```

profile of v0, /device:TPU:0, one launch (start us, length us, event | category | flops | bytes accessed | tf_op | source)
XLA Modules:
  0.0 298.9 jit_solution(16557002799071541110)
XLA Ops:
  7.2 0.0 all-gather.3.cloned.1.call-start
  7.2 0.7 all-gather.3.cloned.1.call-update
  7.9 0.0 all-gather.5.cloned.1.call-start
  7.9 0.7 all-gather.5.cloned.1.call-update
  8.7 1.3 reduce_sum.38
  9.9 0.0 copy-start.1
  9.9 0.0 copy-start.2
  10.0 61.4 %all-gather.3.cloned.1.call-done = bf16[2048,2304]{1,0:T(8,128)(2,1)} async-done(((bf16[256,2304]{1,0:T(8,128)(2,1)}), bf16[2048,2304]{1,0:T(8,128)(2,1)}) %all-gather.3.cloned.1.call-update) | async-done | bytes 9437200 | tf_op jit(solution)/shard_map/all_gather | solution.py:18
  71.3 128.7 %all-gather.5.cloned.1.call-done = bf16[2048,4096]{1,0:T(8,128)(2,1)} async-done(((bf16[128,4096]{1,0:T(8,128)(2,1)}), bf16[2048,4096]{1,0:T(8,128)(2,1)}) %all-gather.5.cloned.1.call-update) | async-done | bytes 16777232 | tf_op jit(solution)/shard_map/all_gather | solution.py:16
  200.0 17.7 %multiply_reduce_fusion.1 = (f32[576]{0:T(1024)S(1)}, f32[4096]{0:T(1024)S(1)}, f32[576,4096]{1,0:T(8,128)}) fusion(bf16[2048,4096]{1,0:T(8,128)(2,1)} %all-gather.5.cloned.1.call-done, bf16[2048,2304]{1,0:T(8,128)(2,1)} %all-gather.3.cloned.1.call-done, s32[]{:T(128)S(6)} %select_n.3), kind=kOutput, calls=%fused_computation.2 | convolution fusion | flops 9673108480 | bytes 28854532 | tf_op jit(solution)/shard_map/dot_general | solution.py:20
  217.7 58.9 %all-reduce = (f32[]{:T(128)}, f32[4096]{0:T(1024)S(1)}) all-reduce(f32[]{:T(128)} %reduce_sum.38, f32[4096]{0:T(1024)S(1)} %get-tuple-element.4), channel_id=1, replica_groups=mesh['outer'=4,'row'=4,'col'=2] {'outer','row'}, use_global_device_ids=true, to_apply=%region_5.0 | all-reduce | flops 4097 | bytes 32776 | tf_op jit(solution)/shard_map/psum | solution.py:23
  276.6 0.0 copy-done.1
  276.6 0.6 multiply_add_fusion
  277.2 0.0 copy-start
  277.2 5.7 %all-reduce.1 = (f32[]{:T(128)}, f32[576]{0:T(1024)S(1)}) all-reduce(f32[]{:T(128)} %get-tuple-element.10, f32[576]{0:T(1024)S(1)} %get-tuple-element.3), channel_id=1, replica_groups=mesh['outer'=4,'row'=4,'col'=2] {'col'}, use_global_device_ids=true, to_apply=%region_7.0 | all-reduce | flops 577 | bytes 4616 | tf_op jit(solution)/shard_map/psum | solution.py:26
  282.9 0.0 copy-done.2
  282.9 0.0 copy-start.3
  284.3 7.8 %multiply_convert_fusion = bf16[576,4096]{1,0:T(8,128)(2,1)} fusion(f32[576,4096]{1,0:T(8,128)} %get-tuple-element.11, f32[]{:T(128)S(6)} %div.23, f32[4096]{0:T(1024)S(1)} %get-tuple-element.9, f32[576]{0:T(1024)S(1)} %multiply_add_fusion.1), kind=kLoop, calls=%fused_computation | loop fusion | flops 11796480 | bytes 14174468 | tf_op jit(solution)/shard_map/convert_element_type | solution.py:32
  292.0 0.0 copy-done
  292.0 0.0 copy-done.3
  (1 shorter events, 0.0 us)
Async XLA Ops:
  7.2 64.1 %all-gather.3.cloned.1.call-start = ((), (), s32[]{:S(2)}) async-start(), calls=%async_computation | async-start | bytes 10616832 | tf_op jit(solution)/shard_map/all_gather | solution.py:18
  7.9 192.1 %all-gather.5.cloned.1.call-start = ((), (), s32[]{:S(2)}) async-start(), calls=%async_computation.1 | async-start | bytes 17825792 | tf_op jit(solution)/shard_map/all_gather | solution.py:16
  9.9 266.6 %copy-start.1 = (f32[4096]{0:T(1024)S(1)}, f32[4096]{0:T(1024)}, u32[]{:S(2)}) copy-start(f32[4096]{0:T(1024)} %param.7) | copy-start | bytes 49156
  9.9 272.9 %copy-start.2 = (f32[576]{0:T(1024)S(1)}, f32[576]{0:T(1024)}, u32[]{:S(2)}) copy-start(f32[576]{0:T(1024)} %param.6) | copy-start | bytes 6916
  277.2 14.9 %copy-start = (f32[4096]{0:T(1024)}, f32[4096]{0:T(1024)S(1)}, u32[]{:S(2)}) copy-start(f32[4096]{0:T(1024)S(1)} %get-tuple-element.9) | copy-start | bytes 49156
  282.9 9.2 %copy-start.3 = (f32[576]{0:T(1024)}, f32[576]{0:T(1024)S(1)}, u32[]{:S(2)}) copy-start(f32[576]{0:T(1024)S(1)} %multiply_add_fusion.1) | copy-start | bytes 6916
Sparse Core Ops, SparseCore 0:
  9.9 61.4 all-gather.2
  73.5 126.4 all-gather.4
where the time goes:
time: 299 us
  waiting for transfers between devices  191 us (64%)
  blocking collectives  64.5 us (22%)
  matrix products  17.7 us (6%)
  between operations  15.4 us (5%)
  other arithmetic  9.68 us (3%)
    all_gather x1, waiting for transfers between devices, body(): grads_all = lax.all_gather(out_grads, ('outer', 'row'), axis=0, tiled=True)  129 us
    all_gather x1, waiting for transfers between devices, body(): lax.all_gather(activations, ('outer', 'col'), axis=0, tiled=True)  61.4 us
    psum x1, blocking collectives, body(): lax.psum((jnp.sum(squares, axis=0), jnp.sum(row_moment)), ('outer', 'row'))  58.9 us
    dot_general x1, matrix products, body(): lax.dot_general(columns, grads_all, contract, preferred_element_type=jnp....  17.7 us
    convert_element_type x1, other arithmetic, body(): update = (gradient * factor).astype(jnp.bfloat16)  7.78 us
  transfers between devices with their start and end apart: 2, of which 2 were waited for; matrix products, arithmetic and copies ran while one was open for 0% of the time, Pallas kernels for 0%

commit v1 on v0

--- a/solution.py
+++ b/solution.py
@@ -1,11 +1,26 @@
+import functools
 import jax
 import jax.numpy as jnp
 from jax import lax
 from jax.sharding import PartitionSpec as P
+from jax.lax import all_to_all, psum
 
 D = 9216
 F = 8192
 STEP = 2
+
+
+def trace_axis_part(array_in, device_axis):
+    heap = []
+    for _ in range(psum(1, axis_name=device_axis)):
+        heap.append(array_in)
+    return jnp.concatenate(
+        all_to_all(jnp.stack(heap, axis=0), split_axis=0, axis_name=device_axis, concat_axis=0),
+        axis=0,
+    )
+
+
+levels_all_raise = functools.partial(trace_axis_part, device_axis=("outer", "col"))
 
 
 def body(activations, out_grads, row_moment, col_moment):
@@ -14,9 +29,7 @@
     token_count = activations.shape[0] * lax.axis_size("col") * lax.axis_size("outer")
     contract = (((0,), (0,)), ((), ()))
     grads_all = lax.all_gather(out_grads, ("outer", "row"), axis=0, tiled=True)
-    columns = lax.dynamic_slice_in_dim(
-        lax.all_gather(activations, ("outer", "col"), axis=0, tiled=True), quarter, row_count, 1
-    )
+    columns = lax.dynamic_slice_in_dim(levels_all_raise(activations), quarter, row_count, 1)
     gradient = lax.dot_general(columns, grads_all, contract, preferred_element_type=jnp.float32)
     gradient = gradient * (1.0 / token_count**0.5)
     squares = gradient * gradient

time: 299 us -> 309 us (1.033)
  local copies, waits for them, and re-layouts: 0.01 us -> 5.52 us
  starting transfers between devices: 0.08 us -> 5.37 us
    all_to_all x0 -> x1, waiting for transfers between devices: none -> 142 us  [trace_axis_part(): all_to_all(jnp.stack(heap, axis=0), split_axis=0, axis_name=device_axis,...]
    all_gather x1, waiting for transfers between devices: 129 us -> 48.4 us  [body(): grads_all = lax.all_gather(out_grads, ('outer', 'row'), axis=0, tiled=True)]
    all_gather x1 -> x0, waiting for transfers between devices: 61.4 us -> none  [body(): lax.all_gather(activations, ('outer', 'col'), axis=0, tiled=True)]
    another operation x0 -> x1, local copies, waits for them, and re-layouts: none -> 5.5 us  [trace_axis_part(): jnp.stack(heap, axis=0)]
    all_to_all x0 -> x1, starting transfers between devices: none -> 5.33 us  [trace_axis_part(): all_to_all(jnp.stack(heap, axis=0), split_axis=0, axis_name=device_axis,...]
  transfers between devices with their start and end apart: 2 -> 2, of which waited for: 2 -> 2; matrix products, arithmetic and copies ran while one was open for 0% -> 2% of each run, Pallas kernels for 0% -> 0%
where the time goes in v1:
time: 309 us; the launch traced here: 308 us
  waiting for transfers between devices  191 us (62%)
  blocking collectives  64.5 us (21%)
  matrix products  17.8 us (6%)
  between operations  15.4 us (5%)
  other arithmetic  8.99 us (3%)
  local copies, waits for them, and re-layouts  5.52 us (2%)
  starting transfers between devices  5.37 us (2%)
    all_to_all x1, waiting for transfers between devices, trace_axis_part(): all_to_all(jnp.stack(heap, axis=0), split_axis=0, axis_name=device_axis,...  142 us
    psum x1, blocking collectives, body(): lax.psum((jnp.sum(squares, axis=0), jnp.sum(row_moment)), ('outer', 'row'))  58.8 us
    all_gather x1, waiting for transfers between devices, body(): grads_all = lax.all_gather(out_grads, ('outer', 'row'), axis=0, tiled=True)  48.4 us
    dot_general x1, matrix products, body(): lax.dot_general(columns, grads_all, contract, preferred_element_type=jnp....  17.8 us
    convert_element_type x1, other arithmetic, body(): update = (gradient * factor).astype(jnp.bfloat16)  7.78 us
  transfers between devices with their start and end apart: 2, of which 2 were waited for; matrix products, arithmetic and copies ran while one was open for 2% of the time, Pallas kernels for 0%

profile of v1, /device:TPU:0, one launch (start us, length us, event | category | flops | bytes accessed | tf_op | source)
XLA Modules:
  0.0 308.2 jit_solution(5789355104361110629)
XLA Ops:
  7.2 0.0 all-gather.2.cloned.1.call-start
  7.2 0.7 all-gather.2.cloned.1.call-update
  7.9 5.5 %stack.2 = bf16[8,256,2304]{2,1,0:T(8,128)(2,1)} broadcast(bf16[256,2304]{1,0:T(8,128)(2,1)} %param.4), dimensions={1,2} | broadcast | bytes 10616832 | tf_op jit(solution)/shard_map/stack | solution.py:18
  13.4 0.0 copy-start.2
  13.4 5.3 %all-to-all-start = ((bf16[8,256,2304]{2,1,0:T(8,128)(2,1)}), bf16[8,256,2304]{2,1,0:T(8,128)(2,1)}, u32[]{:S(2)}, u32[]{:S(2)}) async-start(bf16[8,256,2304]{2,1,0:T(8,128)(2,1)} %stack.2), calls=%async_computation | async-start | bytes 18874368 | tf_op jit(solution)/shard_map/all_to_all | solution.py:18
  18.7 0.0 copy-done.2
  18.7 0.6 reduce_sum.38
  19.3 141.6 %all-to-all-done = bf16[8,256,2304]{2,1,0:T(8,128)(2,1)} async-done(((bf16[8,256,2304]{2,1,0:T(8,128)(2,1)}), bf16[8,256,2304]{2,1,0:T(8,128)(2,1)}, u32[]{:S(2)}, u32[]{:S(2)}) %all-to-all-start) | async-done | bytes 9437216 | tf_op jit(solution)/shard_map/all_to_all | solution.py:18
  160.9 48.4 %all-gather.2.cloned.1.call-done = bf16[2048,4096]{1,0:T(8,128)(2,1)} async-done(((bf16[128,4096]{1,0:T(8,128)(2,1)}), bf16[2048,4096]{1,0:T(8,128)(2,1)}) %all-gather.2.cloned.1.call-update) | async-done | bytes 16777232 | tf_op jit(solution)/shard_map/all_gather | solution.py:31
  209.4 0.0 copy-start.1
  209.4 17.8 %multiply_reduce_fusion.1 = (f32[576]{0:T(1024)S(1)}, f32[4096]{0:T(1024)S(1)}, f32[576,4096]{1,0:T(8,128)}) fusion(bf16[2048,4096]{1,0:T(8,128)(2,1)} %all-gather.2.cloned.1.call-done, bf16[2048,2304]{1,0:T(8,128)(2,1)} %bitcast, s32[]{:T(128)S(6)} %select_n.3), kind=kOutput, calls=%fused_computation.2 | convolution fusion | flops 9673108480 | bytes 28854532 | tf_op jit(solution)/shard_map/dot_general | solution.py:33
  227.1 58.8 %all-reduce = (f32[]{:T(128)}, f32[4096]{0:T(1024)S(1)}) all-reduce(f32[]{:T(128)} %reduce_sum.38, f32[4096]{0:T(1024)S(1)} %get-tuple-element.4), channel_id=1, replica_groups=mesh['outer'=4,'row'=4,'col'=2] {'outer','row'}, use_global_device_ids=true, to_apply=%region_5.0 | all-reduce | flops 4097 | bytes 32776 | tf_op jit(solution)/shard_map/psum | solution.py:36
  285.9 0.0 copy-done.1
  285.9 0.6 multiply_add_fusion
  286.5 0.0 copy-start
  286.5 5.7 %all-reduce.1 = (f32[]{:T(128)}, f32[576]{0:T(1024)S(1)}) all-reduce(f32[]{:T(128)} %get-tuple-element.10, f32[576]{0:T(1024)S(1)} %get-tuple-element.3), channel_id=1, replica_groups=mesh['outer'=4,'row'=4,'col'=2] {'col'}, use_global_device_ids=true, to_apply=%region_7.0 | all-reduce | flops 577 | bytes 4616 | tf_op jit(solution)/shard_map/psum | solution.py:39
  292.2 0.0 copy-start.3
  293.6 7.8 %multiply_convert_fusion = bf16[576,4096]{1,0:T(8,128)(2,1)} fusion(f32[576,4096]{1,0:T(8,128)} %get-tuple-element.11, f32[]{:T(128)S(6)} %div.23, f32[4096]{0:T(1024)S(1)} %get-tuple-element.9, f32[576]{0:T(1024)S(1)} %multiply_add_fusion.1), kind=kLoop, calls=%fused_computation | loop fusion | flops 11796480 | bytes 14174468 | tf_op jit(solution)/shard_map/convert_element_type | solution.py:45
  301.4 0.0 copy-done
  301.4 0.0 copy-done.3
  (1 shorter events, 0.0 us)
Async XLA Ops:
  7.2 202.2 %all-gather.2.cloned.1.call-start = ((), (), s32[]{:S(2)}) async-start(), calls=%async_computation.1 | async-start | bytes 17825792 | tf_op jit(solution)/shard_map/all_gather | solution.py:31
  13.4 5.3 %copy-start.2 = (f32[576]{0:T(1024)S(1)}, f32[576]{0:T(1024)}, u32[]{:S(2)}) copy-start(f32[576]{0:T(1024)} %param.6) | copy-start | bytes 6916
  13.4 147.5 %all-to-all-start = ((bf16[8,256,2304]{2,1,0:T(8,128)(2,1)}), bf16[8,256,2304]{2,1,0:T(8,128)(2,1)}, u32[]{:S(2)}, u32[]{:S(2)}) async-start(bf16[8,256,2304]{2,1,0:T(8,128)(2,1)} %stack.2), calls=%async_computation | async-start | bytes 18874368 | tf_op jit(solution)/shard_map/all_to_all | solution.py:18
  209.4 76.6 %copy-start.1 = (f32[4096]{0:T(1024)S(1)}, f32[4096]{0:T(1024)}, u32[]{:S(2)}) copy-start(f32[4096]{0:T(1024)} %param.7) | copy-start | bytes 49156
  286.5 14.9 %copy-start = (f32[4096]{0:T(1024)}, f32[4096]{0:T(1024)S(1)}, u32[]{:S(2)}) copy-start(f32[4096]{0:T(1024)S(1)} %get-tuple-element.9) | copy-start | bytes 49156
  292.2 9.2 %copy-start.3 = (f32[576]{0:T(1024)}, f32[576]{0:T(1024)S(1)}, u32[]{:S(2)}) copy-start(f32[576]{0:T(1024)S(1)} %multiply_add_fusion.1) | copy-start | bytes 6916
Sparse Core Ops, SparseCore 0:
  10.2 199.1 all-gather.1
